TPU v7x, 256 devices: a whole 4x4x8 slice. The times are simulated.
256 devices in a mesh: dp: 8 (over z_lo, x), expert: 32 (over y, z_hi, core).
Axes of the slice: x: 4, y: 4, z: 8 (z_hi: 4, z_lo: 2; z = z_hi * 2 + z_lo), core: 2. Of those that a mesh axis runs over, the one named last changes fastest.
Arguments:
- tokens: bfloat16 [4096, 7168], P('expert', 'dp'), may hold values from -6 to 6
- cotangent: bfloat16 [4096, 7168], P('expert', 'dp'), may hold values from -6 to 6
- routes: int32 [4096, 4], P('expert'), may hold values from 0 to 31, all different within a row; in each aligned block of 128 rows (0 to 127, 128 to 255, ...) at most 24 rows name the same one
- combine_weights: float32 [4096, 4], P('expert'), may hold values from 0.2 to 1
- gate_weight: bfloat16 [32, 7168, 1024], P('expert', 'dp'), may hold values from -0.0625 to 0.0625
- up_weight: bfloat16 [32, 7168, 1024], P('expert', 'dp'), may hold values from -0.0625 to 0.0625
- down_weight: bfloat16 [32, 1024, 7168], P('expert', None, 'dp'), may hold values from -0.1875 to 0.1875
Outputs:
- grad_tokens: bfloat16 [4096, 7168], P('expert', 'dp')
- grad_gate: bfloat16 [32, 7168, 1024], P('expert', 'dp')
- grad_up: bfloat16 [32, 7168, 1024], P('expert', 'dp')
- grad_down: bfloat16 [32, 1024, 7168], P('expert', None, 'dp')
Inputs may be any that keep to these rules, and one draw needn't show every extreme that they name: `routes`: each row names 4 different experts. Within each aligned block of 128 tokens no expert is named by more than 24 tokens, and in every draw some block has an expert named by exactly 24 tokens.
All inputs are finite; a program needn't handle non-finite values.
Results may differ from a plain program's by a relative error of at most 0.029.
Values may be sent and summed in bfloat16 or wider, within the bound.
No kernel may reach another device: no remote copies, remote signals or barrier semaphores. Data moves between devices by JAX's collectives and lax.ppermute only.
A program may use at most 64 MiB of HBM per device.

v0:
```python
import jax
import jax.numpy as jnp
from jax import lax
from jax.sharding import PartitionSpec as P


def contract(left, right, left_dim, right_dim):
    return lax.dot_general(
        left, right, (((left_dim,), (right_dim,)), ((), ())), preferred_element_type=jnp.float32
    )


def local(tokens, cotangent, routes, combine_weights, gate_weight, up_weight, down_weight):
    experts = lax.axis_size("expert")
    tok_count = routes.shape[0]
    top_count = routes.shape[1]
    width = tokens.shape[1]
    capacity = 3 * tok_count * top_count // (2 * experts)
    flat_routes = routes.reshape(-1)
    onehot = (flat_routes[:, None] == jnp.arange(experts, dtype=jnp.int32)[None, :]).astype(
        jnp.int32
    )
    slot_rank = jnp.sum((jnp.cumsum(onehot, axis=0) - onehot) * onehot, axis=1)
    slots = flat_routes * capacity + slot_rank
    x_pairs = jnp.repeat(tokens, top_count, axis=0)
    scaled = (combine_weights[:, :, None] * cotangent[:, None, :].astype(jnp.float32)).astype(
        jnp.bfloat16
    )
    scaled = scaled.reshape(tok_count * top_count, width)
    empty = jnp.zeros((experts * capacity, width), jnp.bfloat16)
    send_x = empty.at[slots].set(x_pairs).reshape(experts, capacity, width)
    send_s = empty.at[slots].set(scaled).reshape(experts, capacity, width)
    weight_g = gate_weight[0]
    weight_u = up_weight[0]
    weight_d = down_weight[0]
    recv_x, recv_s = (
        lax.all_to_all(send_x, "expert", split_axis=0, concat_axis=0, tiled=True),
        lax.all_to_all(send_s, "expert", split_axis=0, concat_axis=0, tiled=True),
    )
    gate_part = jnp.dot(
        recv_x.reshape(-1, width), weight_g, preferred_element_type=jnp.float32
    ).astype(jnp.bfloat16)
    up_part = jnp.dot(
        recv_x.reshape(-1, width), weight_u, preferred_element_type=jnp.float32
    ).astype(jnp.bfloat16)
    rows_x = recv_x.reshape(-1, width)
    rows_s = recv_s.reshape(-1, width)
    back_part = contract(rows_s, weight_d, 1, 1).astype(jnp.bfloat16)
    gate_share, upper_share = (
        lax.psum_scatter(gate_part, "dp", scatter_dimension=1, tiled=True).astype(jnp.float32),
        lax.psum_scatter(up_part, "dp", scatter_dimension=1, tiled=True).astype(jnp.float32),
    )
    activation = jax.nn.silu(gate_share)
    hidden_share = (activation * upper_share).astype(jnp.bfloat16)
    hidden = lax.all_gather(hidden_share, "dp", axis=1, tiled=True)
    dhidden = lax.psum_scatter(back_part, "dp", scatter_dimension=1, tiled=True).astype(jnp.float32)
    sigmoid_g = jax.nn.sigmoid(gate_share)
    slope = sigmoid_g * (1.0 + gate_share * (1.0 - sigmoid_g))
    gate_grad_share = (dhidden * upper_share * slope).astype(jnp.bfloat16)
    up_grad_share = (dhidden * activation).astype(jnp.bfloat16)
    pre_gate, pre_up = (
        lax.all_gather(gate_grad_share, "dp", axis=1, tiled=True),
        lax.all_gather(up_grad_share, "dp", axis=1, tiled=True),
    )
    back_rows = (contract(pre_gate, weight_g, 1, 1) + contract(pre_up, weight_u, 1, 1)).astype(
        jnp.bfloat16
    )
    returned = lax.all_to_all(
        back_rows.reshape(experts, capacity, width),
        "expert",
        split_axis=0,
        concat_axis=0,
        tiled=True,
    )
    grad_down = contract(hidden, rows_s, 0, 0).astype(jnp.bfloat16)[None]
    grad_gate = contract(rows_x, pre_gate, 0, 0).astype(jnp.bfloat16)[None]
    grad_up = contract(rows_x, pre_up, 0, 0).astype(jnp.bfloat16)[None]
    picked = returned.reshape(experts * capacity, width)[slots]
    grad_tokens = jnp.sum(
        picked.reshape(tok_count, top_count, width).astype(jnp.float32), axis=1
    ).astype(jnp.bfloat16)
    return (grad_tokens, grad_gate, grad_up, grad_down)


def solution(mesh):
    placed = (
        P("expert", "dp"),
        P("expert", "dp"),
        P("expert", None),
        P("expert", None),
        P("expert", "dp", None),
        P("expert", "dp", None),
        P("expert", None, "dp"),
    )
    return jax.shard_map(
        local,
        mesh=mesh,
        in_specs=placed,
        out_specs=(
            P("expert", "dp"),
            P("expert", "dp", None),
            P("expert", "dp", None),
            P("expert", None, "dp"),
        ),
        check_vma=False,
    )
```

profile of v0, /device:TPU:1, one launch (start us, length us, event | category | flops | bytes accessed | tf_op | source)
XLA Modules:
  0.0 386.5 jit_solution(345836730867990617)
XLA Ops:
  13.1 3.5 scatter_custom_fusion.1
  16.7 49.8 %all_to_all.15 = bf16[32,24,896]{2,1,0:T(8,128)(2,1)S(1)} all-to-all(bf16[32,24,896]{2,1,0:T(8,128)(2,1)S(1)} %bitcast.76), channel_id=1, replica_groups=mesh['dp'=8,'expert'=32] {'expert'}, dimensions={0} | all-to-all | bytes 2752512 | tf_op jit(solution)/shard_map/all_to_all | solution.py:37
  67.7 1.8 fusion.13
  69.5 1.6 copy.23
  71.1 3.1 fusion.16
  74.3 1.6 copy.25
  78.3 2.8 mul.66
  81.3 3.9 %scatter_custom_fusion = bf16[768,896]{1,0:T(8,128)(2,1)S(1)} fusion(s32[512]{0:T(512)S(1)} %bitcast.88, f32[512,896]{1,0:T(8,128)} %mul.66, f32[512]{0:T(512)S(1)} %mul.63, bf16[]{:T(256)} %constant.5.clone.1), kind=kCustom, calls=%fused_computation.21 | custom fusion | flops 917504 | bytes 3213314 | tf_op jit(solution)/shard_map/scatter | solution.py:32
  85.3 48.7 %all_to_all.16 = bf16[32,24,896]{2,1,0:T(8,128)(2,1)S(1)} all-to-all(bf16[32,24,896]{2,1,0:T(8,128)(2,1)S(1)} %bitcast.75), channel_id=1, replica_groups=mesh['dp'=8,'expert'=32] {'expert'}, dimensions={0} | all-to-all | bytes 2752512 | tf_op jit(solution)/shard_map/all_to_all | solution.py:38
  135.1 1.8 fusion.10
  139.7 22.9 %reduce-scatter.14.cloned.1.call-done = bf16[128,768]{1,0:T(8,128)(2,1)} async-done(((bf16[1024,768]{1,0:T(8,128)(2,1)}), bf16[128,768]{1,0:T(8,128)(2,1)}) %reduce-scatter.14.cloned.1.call-update) | async-done | bytes 196624
  163.7 44.3 %reduce-scatter.10.cloned.1.call-done = bf16[128,768]{1,0:T(8,128)(2,1)} async-done(((bf16[1024,768]{1,0:T(8,128)(2,1)}), bf16[128,768]{1,0:T(8,128)(2,1)}) %reduce-scatter.10.cloned.1.call-update) | async-done | bytes 196624
  211.3 42.8 %all-gather.4.cloned.1.call-done = bf16[768,1024]{1,0:T(8,128)(2,1)} async-done(((bf16[768,128]{1,0:T(8,128)(2,1)}), bf16[768,1024]{1,0:T(8,128)(2,1)}) %all-gather.4.cloned.1.call-update) | async-done | bytes 1572880 | tf_op jit(solution)/shard_map/all_gather | solution.py:62
  254.1 4.8 %fusion = f32[768,896]{1,0:T(8,128)} fusion(bf16[768,1024]{1,0:T(8,128)(2,1)} %all-gather.4.cloned.1.call-done, bf16[1,896,1024]{2,1,0:T(8,128)(2,1)S(1)} %copy-done), kind=kOutput, calls=%fused_computation.4 | convolution fusion | flops 1409286144 | bytes 6160384 | tf_op jit(solution)/shard_map/dot_general | solution.py:8
  258.9 42.3 %all-gather.6.cloned.1.call-done = bf16[768,1024]{1,0:T(8,128)(2,1)} async-done(((bf16[768,128]{1,0:T(8,128)(2,1)}), bf16[768,1024]{1,0:T(8,128)(2,1)}) %all-gather.6.cloned.1.call-update) | async-done | bytes 1572880 | tf_op jit(solution)/shard_map/all_gather | solution.py:63
  301.3 5.7 %add_convert_fusion = bf16[768,896]{1,0:T(8,128)(2,1)} fusion(f32[768,896]{1,0:T(8,128)} %fusion, bf16[768,1024]{1,0:T(8,128)(2,1)} %all-gather.6.cloned.1.call-done, bf16[1,896,1024]{2,1,0:T(8,128)(2,1)} %param.12), kind=kOutput, calls=%fused_computation.3 | convolution fusion | flops 1410662400 | bytes 7536640 | tf_op jit(solution)/shard_map/dot_general | solution.py:8
  307.0 14.1 %all-to-all-start.2 = ((bf16[32,24,896]{2,1,0:T(8,128)(2,1)}), bf16[32,24,896]{2,1,0:T(8,128)(2,1)S(1)}, u32[]{:S(2)}, u32[]{:S(2)}) async-start(bf16[32,24,896]{2,1,0:T(8,128)(2,1)} %bitcast.83), calls=%async_computation.2 | async-start | bytes 2752512 | tf_op jit(solution)/shard_map/all_to_all | solution.py:68
  321.1 4.8 %convert_bitcast_fusion.1 = bf16[1,896,1024]{2,1,0:T(8,128)(2,1)} fusion(bf16[768,896]{1,0:T(8,128)(2,1)} %bitcast.79, bf16[768,1024]{1,0:T(8,128)(2,1)} %all-gather.6.cloned.1.call-done), kind=kOutput, calls=%fused_computation.15 | convolution fusion | flops 1410203648 | bytes 4784128 | tf_op jit(solution)/shard_map/dot_general | solution.py:8
  325.9 2.9 convert_bitcast_fusion.2
  328.8 39.6 %all-gather.8.cloned.1.call-done = bf16[768,1024]{1,0:T(8,128)(2,1)} async-done(((bf16[768,128]{1,0:T(8,128)(2,1)}), bf16[768,1024]{1,0:T(8,128)(2,1)}) %all-gather.8.cloned.1.call-update) | async-done | bytes 1572880 | tf_op jit(solution)/shard_map/all_gather | solution.py:55
  368.4 4.9 %convert_bitcast_fusion = bf16[1,1024,896]{2,1,0:T(8,128)(2,1)} fusion(bf16[768,1024]{1,0:T(8,128)(2,1)} %all-gather.8.cloned.1.call-done, bf16[768,896]{1,0:T(8,128)(2,1)} %bitcast.82), kind=kOutput, calls=%fused_computation.14 | convolution fusion | flops 1410203648 | bytes 4784128 | tf_op jit(solution)/shard_map/dot_general | solution.py:8
  373.3 2.7 gather_fusion
  376.0 1.8 reshape.95
  377.8 1.9 reduce_sum.25
  (56 shorter events, 18.0 us)
Async XLA Ops:
  7.2 64.0 %copy-start = (bf16[1,896,1024]{2,1,0:T(8,128)(2,1)S(1)}, bf16[1,896,1024]{2,1,0:T(8,128)(2,1)}, u32[]{:S(2)}) copy-start(bf16[1,896,1024]{2,1,0:T(8,128)(2,1)} %param.11) | copy-start | bytes 5505028
  7.2 131.4 %reduce-scatter.12.cloned.1.call-start = ((), (), s32[]{:S(2)}) async-start(), calls=%async_computation.10 | async-start | bytes 1769472
  16.7 51.0 %copy-start.7 = (bf16[1,896,1024]{2,1,0:T(8,128)(2,1)S(1)}, bf16[1,896,1024]{2,1,0:T(8,128)(2,1)}, u32[]{:S(2)}) copy-start(bf16[1,896,1024]{2,1,0:T(8,128)(2,1)} %param.12) | copy-start | bytes 5505028
  66.5 1.2 copy-start.1
  71.1 91.6 %reduce-scatter.14.cloned.1.call-start = ((), (), s32[]{:S(2)}) async-start(), calls=%async_computation.11 | async-start | bytes 1769472
  75.9 0.9 copy-start.4
  75.9 132.1 %reduce-scatter.10.cloned.1.call-start = ((), (), s32[]{:S(2)}) async-start(), calls=%async_computation.9 | async-start | bytes 1769472
  78.3 2.9 copy-start.5
  85.3 49.8 %copy-start.6 = (bf16[1,1024,896]{2,1,0:T(8,128)(2,1)S(1)}, bf16[1,1024,896]{2,1,0:T(8,128)(2,1)}, u32[]{:S(2)}) copy-start(bf16[1,1024,896]{2,1,0:T(8,128)(2,1)} %param.13) | copy-start | bytes 5505028
  133.9 1.1 copy-start.3
  138.5 115.6 %all-gather.4.cloned.1.call-start = ((), (), s32[]{:S(2)}) async-start(), calls=%async_computation.6 | async-start | bytes 1769472 | tf_op jit(solution)/shard_map/all_gather | solution.py:62
  210.2 91.1 %all-gather.6.cloned.1.call-start = ((), (), s32[]{:S(2)}) async-start(), calls=%async_computation.7 | async-start | bytes 1769472 | tf_op jit(solution)/shard_map/all_gather | solution.py:63
  210.8 157.6 %all-gather.8.cloned.1.call-start = ((), (), s32[]{:S(2)}) async-start(), calls=%async_computation.8 | async-start | bytes 1769472 | tf_op jit(solution)/shard_map/all_gather | solution.py:55
  307.0 66.3 %all-to-all-start.2 = ((bf16[32,24,896]{2,1,0:T(8,128)(2,1)}), bf16[32,24,896]{2,1,0:T(8,128)(2,1)S(1)}, u32[]{:S(2)}, u32[]{:S(2)}) async-start(bf16[32,24,896]{2,1,0:T(8,128)(2,1)} %bitcast.83), calls=%async_computation.2 | async-start | bytes 2752512 | tf_op jit(solution)/shard_map/all_to_all | solution.py:68
  321.1 4.8 %copy-start.2 = (bf16[32,24,896]{2,1,0:T(8,128)(2,1)S(1)}, bf16[32,24,896]{2,1,0:T(8,128)(2,1)}, u32[]{:S(2)}) copy-start(bf16[32,24,896]{2,1,0:T(8,128)(2,1)} %copy-done.1) | copy-start | bytes 4128772
  321.1 4.8 %copy-start.8 = (bf16[768,1024]{1,0:T(8,128)(2,1)S(1)}, bf16[768,1024]{1,0:T(8,128)(2,1)}, u32[]{:S(2)}) copy-start(bf16[768,1024]{1,0:T(8,128)(2,1)} %all-gather.4.cloned.1.call-done) | copy-start | bytes 4718596
Sparse Core Ops, SparseCore 0:
  71.2 48.9 reduce-scatter.11
  122.7 39.8 reduce-scatter.13
  165.8 42.2 reduce-scatter.9
  210.3 43.8 all-gather.3
  256.3 44.9 all-gather.5
  303.4 64.9 all-gather.7
where the time goes:
time: 387 us
  waiting for transfers between devices  193 us (50%)
  blocking collectives  98.5 us (25%)
  matrix products  29.8 us (8%)
  local copies, waits for them, and re-layouts  27.7 us (7%)
  starting transfers between devices  14.3 us (4%)
  between operations  14.3 us (4%)
  other arithmetic  8.87 us (2%)
    unnamed x9, waiting for transfers between devices  68.4 us
    all_to_all x1, blocking collectives, local(): lax.all_to_all(send_x, 'expert', split_axis=0, concat_axis=0, tiled=True)  49.8 us
    all_to_all x1, blocking collectives, local(): lax.all_to_all(send_s, 'expert', split_axis=0, concat_axis=0, tiled=True)  48.7 us
    all_gather x1, waiting for transfers between devices, local(): lax.all_gather(gate_grad_share, 'dp', axis=1, tiled=True)  42.8 us
    all_gather x1, waiting for transfers between devices, local(): lax.all_gather(up_grad_share, 'dp', axis=1, tiled=True)  42.3 us
    all_gather x1, waiting for transfers between devices, local(): hidden = lax.all_gather(hidden_share, 'dp', axis=1, tiled=True)  39.6 us
    dot_general x6, matrix products, contract(): lax.dot_general(left, right, (((left_dim,), (right_dim,)), ((), ())), pre...  24.9 us
    all_to_all x1, starting transfers between devices, local(): lax.all_to_all(back_rows.reshape(experts, capacity, width), 'expert', spl...  14.1 us
  transfers between devices with their start and end apart: 7, of which 5 were waited for; matrix products, arithmetic and copies ran while one was open for 11% of the time, Pallas kernels for 0%

commit v1 on v0

--- a/solution.py
+++ b/solution.py
@@ -2,6 +2,7 @@
 import jax.numpy as jnp
 from jax import lax
 from jax.sharding import PartitionSpec as P
+from jax.lax import all_to_all, axis_size
 
 
 def contract(left, right, left_dim, right_dim):
@@ -58,9 +59,18 @@
     slope = sigmoid_g * (1.0 + gate_share * (1.0 - sigmoid_g))
     gate_grad_share = (dhidden * upper_share * slope).astype(jnp.bfloat16)
     up_grad_share = (dhidden * activation).astype(jnp.bfloat16)
+    report_the_frames = lambda u_in, k_dim: jnp.concatenate(
+        all_to_all(
+            jnp.stack([u_in for _ in range(axis_size("dp"))], axis=0),
+            "dp",
+            split_axis=0,
+            concat_axis=0,
+        ),
+        axis=k_dim,
+    )
     pre_gate, pre_up = (
         lax.all_gather(gate_grad_share, "dp", axis=1, tiled=True),
-        lax.all_gather(up_grad_share, "dp", axis=1, tiled=True),
+        report_the_frames(up_grad_share, 1),
     )
     back_rows = (contract(pre_gate, weight_g, 1, 1) + contract(pre_up, weight_u, 1, 1)).astype(
         jnp.bfloat16

time: 387 us -> 347 us (0.90)
  waiting for transfers between devices: 193 us -> 147 us
    all_gather x1 -> x0, waiting for transfers between devices: 42.3 us -> none  [local(): lax.all_gather(up_grad_share, 'dp', axis=1, tiled=True)]
    all_gather x1, waiting for transfers between devices: 39.6 us -> 32.8 us  [local(): hidden = lax.all_gather(hidden_share, 'dp', axis=1, tiled=True)]
    unnamed x9 -> x8, waiting for transfers between devices: 68.4 us -> 68 us
    unnamed x26 -> x28, local copies, waits for them, and re-layouts: 12.2 us -> 12.2 us
  transfers between devices with their start and end apart: 7 -> 7, of which waited for: 5 -> 5; matrix products, arithmetic and copies ran while one was open for 11% -> 13% of each run, Pallas kernels for 0% -> 0%
where the time goes in v1:
time: 347 us; the launch traced here: 345 us
  waiting for transfers between devices  147 us (42%)
  blocking collectives  98.5 us (28%)
  matrix products  30.1 us (9%)
  local copies, waits for them, and re-layouts  29 us (8%)
  starting transfers between devices  17.9 us (5%)
  between operations  14 us (4%)
  other arithmetic  8.84 us (3%)
    unnamed x8, waiting for transfers between devices  68 us
    all_to_all x1, blocking collectives, local(): lax.all_to_all(send_x, 'expert', split_axis=0, concat_axis=0, tiled=True)  49.8 us
    all_to_all x1, blocking collectives, local(): lax.all_to_all(send_s, 'expert', split_axis=0, concat_axis=0, tiled=True)  48.7 us
    all_gather x1, waiting for transfers between devices, local(): lax.all_gather(gate_grad_share, 'dp', axis=1, tiled=True)  44.4 us
    all_gather x1, waiting for transfers between devices, local(): hidden = lax.all_gather(hidden_share, 'dp', axis=1, tiled=True)  32.8 us
    dot_general x6, matrix products, contract(): lax.dot_general(left, right, (((left_dim,), (right_dim,)), ((), ())), pre...  25.2 us
    all_to_all x1, starting transfers between devices, local(): lax.all_to_all(back_rows.reshape(experts, capacity, width), 'expert', spl...  13.9 us
    unnamed x28, local copies, waits for them, and re-layouts  12.2 us
  transfers between devices with their start and end apart: 7, of which 5 were waited for; matrix products, arithmetic and copies ran while one was open for 13% of the time, Pallas kernels for 0%

profile of v1, /device:TPU:1, one launch (start us, length us, event | category | flops | bytes accessed | tf_op | source)
XLA Modules:
  0.0 345.4 jit_solution(4102823642528729209)
XLA Ops:
  13.1 3.5 %scatter_custom_fusion.1 = bf16[768,896]{1,0:T(8,128)(2,1)S(1)} fusion(s32[512]{0:T(512)S(1)} %bitcast.92, bf16[512,896]{1,0:T(8,128)(2,1)} %reshape.126, bf16[]{:T(256)} %constant.5.clone.1), kind=kCustom, calls=%fused_computation.23 | custom fusion | bytes 1376768 | tf_op jit(solution)/shard_map/scatter | solution.py:32
  16.7 49.8 %all_to_all.20 = bf16[32,24,896]{2,1,0:T(8,128)(2,1)S(1)} all-to-all(bf16[32,24,896]{2,1,0:T(8,128)(2,1)S(1)} %bitcast.79), channel_id=1, replica_groups=mesh['dp'=8,'expert'=32] {'expert'}, dimensions={0} | all-to-all | bytes 2752512 | tf_op jit(solution)/shard_map/all_to_all | solution.py:38
  67.6 1.8 fusion.13
  71.1 3.1 fusion.16
  74.2 1.6 copy.27
  78.2 2.8 mul.66
  81.3 3.9 %scatter_custom_fusion = bf16[768,896]{1,0:T(8,128)(2,1)S(1)} fusion(s32[512]{0:T(512)S(1)} %bitcast.93, f32[512,896]{1,0:T(8,128)} %mul.66, f32[512]{0:T(512)S(1)} %mul.63, bf16[]{:T(256)} %constant.5.clone.1), kind=kCustom, calls=%fused_computation.21 | custom fusion | flops 917504 | bytes 3213314 | tf_op jit(solution)/shard_map/scatter | solution.py:33
  85.2 48.7 %all_to_all.21 = bf16[32,24,896]{2,1,0:T(8,128)(2,1)S(1)} all-to-all(bf16[32,24,896]{2,1,0:T(8,128)(2,1)S(1)} %bitcast.78), channel_id=1, replica_groups=mesh['dp'=8,'expert'=32] {'expert'}, dimensions={0} | all-to-all | bytes 2752512 | tf_op jit(solution)/shard_map/all_to_all | solution.py:39
  135.1 1.8 fusion.10
  139.6 23.1 %reduce-scatter.14.cloned.1.call-done = bf16[128,768]{1,0:T(8,128)(2,1)} async-done(((bf16[1024,768]{1,0:T(8,128)(2,1)}), bf16[128,768]{1,0:T(8,128)(2,1)}) %reduce-scatter.14.cloned.1.call-update) | async-done | bytes 196624
  163.8 44.3 %reduce-scatter.10.cloned.1.call-done = bf16[128,768]{1,0:T(8,128)(2,1)} async-done(((bf16[1024,768]{1,0:T(8,128)(2,1)}), bf16[128,768]{1,0:T(8,128)(2,1)}) %reduce-scatter.10.cloned.1.call-update) | async-done | bytes 196624
  211.6 3.8 %all-to-all-start.2 = ((bf16[8,768,128]{1,2,0:T(8,128)(2,1)}), bf16[8,768,128]{1,2,0:T(8,128)(2,1)S(1)}, u32[]{:S(2)}, u32[]{:S(2)}) async-start(bf16[8,768,128]{1,2,0:T(8,128)(2,1)} %stack.2), calls=%async_computation.2 | async-start | bytes 3145728 | tf_op jit(solution)/shard_map/all_to_all | solution.py:63
  216.0 44.4 %all-gather.3.cloned.1.call-done = bf16[768,1024]{1,0:T(8,128)(2,1)} async-done(((bf16[768,128]{1,0:T(8,128)(2,1)}), bf16[768,1024]{1,0:T(8,128)(2,1)}) %all-gather.3.cloned.1.call-update) | async-done | bytes 1572880 | tf_op jit(solution)/shard_map/all_gather | solution.py:72
  260.4 4.8 %fusion = f32[768,896]{1,0:T(8,128)} fusion(bf16[768,1024]{1,0:T(8,128)(2,1)} %all-gather.3.cloned.1.call-done, bf16[1,896,1024]{2,1,0:T(8,128)(2,1)S(1)} %copy-done), kind=kOutput, calls=%fused_computation.4 | convolution fusion | flops 1409286144 | bytes 6160384 | tf_op jit(solution)/shard_map/dot_general | solution.py:9
  265.2 5.9 %add_convert_fusion = bf16[768,896]{1,0:T(8,128)(2,1)} fusion(f32[768,896]{1,0:T(8,128)} %fusion, bf16[768,1024]{0,1:T(8,128)(2,1)S(1)} %bitcast.80, bf16[1,896,1024]{2,1,0:T(8,128)(2,1)} %param.12), kind=kOutput, calls=%fused_computation.3 | convolution fusion | flops 1410662400 | bytes 7536640 | tf_op jit(solution)/shard_map/dot_general | solution.py:9
  271.1 13.9 %all-to-all-start.3 = ((bf16[32,24,896]{2,1,0:T(8,128)(2,1)}), bf16[32,24,896]{2,1,0:T(8,128)(2,1)S(1)}, u32[]{:S(2)}, u32[]{:S(2)}) async-start(bf16[32,24,896]{2,1,0:T(8,128)(2,1)} %bitcast.88), calls=%async_computation.3 | async-start | bytes 2752512 | tf_op jit(solution)/shard_map/all_to_all | solution.py:78
  285.0 4.9 %convert_bitcast_fusion.1 = bf16[1,896,1024]{2,1,0:T(8,128)(2,1)} fusion(bf16[768,896]{1,0:T(8,128)(2,1)} %bitcast.84, bf16[768,1024]{0,1:T(8,128)(2,1)} %bitcast.81), kind=kOutput, calls=%fused_computation.15 | convolution fusion | flops 1410203648 | bytes 4784128 | tf_op jit(solution)/shard_map/dot_general | solution.py:9
  290.0 2.9 convert_bitcast_fusion.2
  292.8 32.8 %all-gather.5.cloned.1.call-done = bf16[768,1024]{1,0:T(8,128)(2,1)} async-done(((bf16[768,128]{1,0:T(8,128)(2,1)}), bf16[768,1024]{1,0:T(8,128)(2,1)}) %all-gather.5.cloned.1.call-update) | async-done | bytes 1572880 | tf_op jit(solution)/shard_map/all_gather | solution.py:56
  325.7 4.9 %convert_bitcast_fusion = bf16[1,1024,896]{2,1,0:T(8,128)(2,1)} fusion(bf16[768,1024]{1,0:T(8,128)(2,1)} %all-gather.5.cloned.1.call-done, bf16[768,896]{1,0:T(8,128)(2,1)} %bitcast.87), kind=kOutput, calls=%fused_computation.14 | convolution fusion | flops 1410203648 | bytes 4784128 | tf_op jit(solution)/shard_map/dot_general | solution.py:9
  330.5 2.0 all-to-all-done.3
  332.5 2.7 gather_fusion
  335.2 1.8 reshape.105
  337.0 1.9 reduce_sum.25
  (59 shorter events, 20.4 us)
Async XLA Ops:
  7.2 63.9 %copy-start = (bf16[1,896,1024]{2,1,0:T(8,128)(2,1)S(1)}, bf16[1,896,1024]{2,1,0:T(8,128)(2,1)}, u32[]{:S(2)}) copy-start(bf16[1,896,1024]{2,1,0:T(8,128)(2,1)} %param.11) | copy-start | bytes 5505028
  7.2 131.4 %reduce-scatter.12.cloned.1.call-start = ((), (), s32[]{:S(2)}) async-start(), calls=%async_computation.10 | async-start | bytes 1769472
  16.7 50.9 %copy-start.8 = (bf16[1,896,1024]{2,1,0:T(8,128)(2,1)S(1)}, bf16[1,896,1024]{2,1,0:T(8,128)(2,1)}, u32[]{:S(2)}) copy-start(bf16[1,896,1024]{2,1,0:T(8,128)(2,1)} %param.12) | copy-start | bytes 5505028
  66.5 1.1 copy-start.2
  71.0 91.7 %reduce-scatter.14.cloned.1.call-start = ((), (), s32[]{:S(2)}) async-start(), calls=%async_computation.11 | async-start | bytes 1769472
  75.8 0.9 copy-start.5
  75.8 132.3 %reduce-scatter.10.cloned.1.call-start = ((), (), s32[]{:S(2)}) async-start(), calls=%async_computation.9 | async-start | bytes 1769472
  78.2 2.9 copy-start.6
  85.2 49.8 %copy-start.7 = (bf16[1,1024,896]{2,1,0:T(8,128)(2,1)S(1)}, bf16[1,1024,896]{2,1,0:T(8,128)(2,1)}, u32[]{:S(2)}) copy-start(bf16[1,1024,896]{2,1,0:T(8,128)(2,1)} %param.13) | copy-start | bytes 5505028
  133.9 1.1 copy-start.4
  138.5 121.9 %all-gather.3.cloned.1.call-start = ((), (), s32[]{:S(2)}) async-start(), calls=%async_computation.7 | async-start | bytes 1769472 | tf_op jit(solution)/shard_map/all_gather | solution.py:72
  211.6 53.6 %all-to-all-start.2 = ((bf16[8,768,128]{1,2,0:T(8,128)(2,1)}), bf16[8,768,128]{1,2,0:T(8,128)(2,1)S(1)}, u32[]{:S(2)}, u32[]{:S(2)}) async-start(bf16[8,768,128]{1,2,0:T(8,128)(2,1)} %stack.2), calls=%async_computation.2 | async-start | bytes 3145728 | tf_op jit(solution)/shard_map/all_to_all | solution.py:63
  215.4 110.3 %all-gather.5.cloned.1.call-start = ((), (), s32[]{:S(2)}) async-start(), calls=%async_computation.8 | async-start | bytes 1769472 | tf_op jit(solution)/shard_map/all_gather | solution.py:56
  265.2 5.9 %copy-start.1 = (bf16[8,768,128]{1,2,0:T(8,128)(2,1)}, bf16[8,768,128]{1,2,0:T(8,128)(2,1)S(1)}, u32[]{:S(2)}) copy-start(bf16[8,768,128]{1,2,0:T(8,128)(2,1)S(1)} %all-to-all-done.2) | copy-start | bytes 4718596
  271.1 61.4 %all-to-all-start.3 = ((bf16[32,24,896]{2,1,0:T(8,128)(2,1)}), bf16[32,24,896]{2,1,0:T(8,128)(2,1)S(1)}, u32[]{:S(2)}, u32[]{:S(2)}) async-start(bf16[32,24,896]{2,1,0:T(8,128)(2,1)} %bitcast.88), calls=%async_computation.3 | async-start | bytes 2752512 | tf_op jit(solution)/shard_map/all_to_all | solution.py:78
  285.0 4.9 %copy-start.3 = (bf16[32,24,896]{2,1,0:T(8,128)(2,1)S(1)}, bf16[32,24,896]{2,1,0:T(8,128)(2,1)}, u32[]{:S(2)}) copy-start(bf16[32,24,896]{2,1,0:T(8,128)(2,1)} %copy-done.2) | copy-start | bytes 4128772
  285.0 4.9 %copy-start.9 = (bf16[768,1024]{1,0:T(8,128)(2,1)S(1)}, bf16[768,1024]{1,0:T(8,128)(2,1)}, u32[]{:S(2)}) copy-start(bf16[768,1024]{1,0:T(8,128)(2,1)} %all-gather.3.cloned.1.call-done) | copy-start | bytes 4718596
Sparse Core Ops, SparseCore 0:
  71.1 49.0 reduce-scatter.11
  122.7 39.9 reduce-scatter.13
  165.9 42.1 reduce-scatter.9
  210.3 49.9 all-gather.2
  262.5 63.1 all-gather.4
